TPU v7x, 32 devices: a whole 2x2x4 slice. The times are simulated.
32 devices in a mesh: row: 4 (over y, x), col: 8 (over z, core).
Axes of the slice: x: 2, y: 2, z: 4, core: 2. Of those that a mesh axis runs over, the one named last changes fastest.
Arguments:
- new_row: float32 [128, 96, 128], P('row', 'col'), may hold values from -4 to 4
- history: float32 [96, 96, 128, 128], P('row', 'col'), may hold values from -0.0546875 to 0.0546875
- hamiltonian: float32 [128, 128], replicated, may hold values from -0.5 to 0.5
Outputs:
- rows_out: float32 [3, 128, 96, 128], P(None, 'row', 'col')
All inputs are finite; a program needn't handle non-finite values.
Results may differ from a plain program's by a relative error of at most 0.00026.
Values sent between devices are 32-bit elements; how exact they have to be, the bound alone decides.
No kernel may reach another device: no remote copies, remote signals or barrier semaphores. Data moves between devices by JAX's collectives and lax.ppermute only.
A program may use at most 128 MiB of HBM per device.

v0:
```python
import jax
import jax.numpy as jnp
from jax import lax
from jax.sharding import PartitionSpec as P

STEPS = 3
time_step = 0.2


def sigma_panel(sigma_all, tile_rows):
    row_start = lax.axis_index("row") * tile_rows
    pieces = lax.all_to_all(sigma_all, "col", split_axis=0, concat_axis=1, tiled=True)
    needed = lax.dynamic_slice_in_dim(pieces, row_start, tile_rows, 1)
    return lax.all_gather(needed, "col", axis=0, tiled=True)


def contract(sigma_rows, history):
    return jnp.einsum(
        "isl,stlj->itj",
        sigma_rows,
        history,
        precision=lax.Precision.HIGHEST,
        preferred_element_type=jnp.float32,
    )


def advance(current, hamiltonian, collision):
    kinetic = jnp.einsum(
        "itl,lj->itj",
        current,
        hamiltonian,
        precision=lax.Precision.HIGHEST,
        preferred_element_type=jnp.float32,
    )
    return current - time_step * (kinetic + collision)


def per_device(new_row, history, hamiltonian):
    tile_rows = history.shape[0]
    results = []
    current = new_row
    for step_index in range(STEPS):
        sigma_local = current * current * current
        sigma_all = lax.all_gather(sigma_local, "row", axis=0, tiled=True)
        sigma_rows = sigma_panel(sigma_all, tile_rows)
        collision = lax.psum_scatter(
            contract(sigma_rows, history), "row", scatter_dimension=0, tiled=True
        )
        current = advance(current, hamiltonian, collision)
        results.append(current)
    return jnp.stack(results)


def solution(mesh):
    placed = (P("row", "col", None), P("row", "col", None, None), P())
    return jax.shard_map(
        per_device,
        mesh=mesh,
        in_specs=placed,
        out_specs=P(None, "row", "col", None),
        check_vma=False,
    )
```

profile of v0, /device:TPU:0, one launch (start us, length us, event | category | flops | bytes accessed | tf_op | source)
XLA Modules:
  0.0 342.0 jit_solution(1827196471069993955)
XLA Ops:
  6.5 0.0 copy-start
  6.5 1.0 multiply_multiply_fusion.2
  7.5 12.7 %all_gather.18 = f32[128,12,128]{2,0,1:T(8,128)S(1)} all-gather(f32[32,12,128]{2,0,1:T(8,128)S(1)} %multiply_multiply_fusion.2), channel_id=1, replica_groups=mesh['row'=4,'col'=8] {'row'}, dimensions={0}, use_global_device_ids=true | all-gather | bytes 983040 | tf_op jit(solution)/shard_map/all_gather | solution.py:44
  20.2 1.5 copy.21
  21.6 4.9 %all-to-all-start = ((f32[128,12,128]{2,1,0:T(8,128)}), f32[128,12,128]{2,1,0:T(8,128)S(1)}, u32[]{:S(2)}, u32[]{:S(2)}) async-start(f32[128,12,128]{2,1,0:T(8,128)} %copy.21), calls=%async_computation | async-start | bytes 2097152 | tf_op jit(solution)/shard_map/all_to_all | solution.py:12
  26.5 0.0 all-gather.4.cloned.1.call-start
  26.6 26.5 %all-to-all-done = f32[128,12,128]{2,1,0:T(8,128)S(1)} async-done(((f32[128,12,128]{2,1,0:T(8,128)}), f32[128,12,128]{2,1,0:T(8,128)S(1)}, u32[]{:S(2)}, u32[]{:S(2)}) %all-to-all-start) | async-done | bytes 786464 | tf_op jit(solution)/shard_map/all_to_all | solution.py:12
  53.1 0.2 copy.22
  53.3 0.7 constant_dynamic-slice_fusion.2
  54.0 0.0 all-gather.4.cloned.1.call-update
  54.1 0.0 copy-start.1
  54.1 0.0 reduce-scatter.4.cloned.1.call-start
  54.1 23.3 %all-gather.4.cloned.1.call-done = f32[128,24,128]{2,0,1:T(8,128)} async-done(((f32[16,24,128]{2,0,1:T(8,128)}), f32[128,24,128]{2,0,1:T(8,128)}) %all-gather.4.cloned.1.call-update) | async-done | bytes 1572880 | tf_op jit(solution)/shard_map/all_gather | solution.py:14
  77.5 14.3 %fusion.6 = f32[128,12,128]{2,0,1:T(8,128)} fusion(f32[24,12,128,128]{3,2,1,0:T(8,128)} %param.4, f32[128,24,128]{2,0,1:T(8,128)} %all-gather.4.cloned.1.call-done), kind=kOutput, calls=%fused_computation.6 | convolution fusion | flops 7247757312 | bytes 21233664 | tf_op jit(solution)/shard_map/isl,stlj->itj/dot_general | solution.py:18
  91.7 0.0 reduce-scatter.4.cloned.1.call-update
  91.7 0.0 all-gather.6.cloned.1.call-start
  91.8 25.4 %reduce-scatter.4.cloned.1.call-done = f32[32,12,128]{2,0,1:T(8,128)} async-done(((f32[128,12,128]{2,0,1:T(8,128)}), f32[32,12,128]{2,0,1:T(8,128)}) %reduce-scatter.4.cloned.1.call-update) | async-done | bytes 196624 | tf_op jit(solution)/shard_map/reduce_scatter | solution.py:46
  117.2 0.0 copy-done
  117.2 0.0 copy-done.1
  117.2 1.2 multiply_multiply_fusion.1
  118.4 11.2 %all_gather.20 = f32[128,12,128]{2,0,1:T(8,128)S(1)} all-gather(f32[32,12,128]{2,0,1:T(8,128)S(1)} %get-tuple-element.5), channel_id=1, replica_groups=mesh['row'=4,'col'=8] {'row'}, dimensions={0}, use_global_device_ids=true | all-gather | bytes 983040 | tf_op jit(solution)/shard_map/all_gather | solution.py:44
  129.6 0.5 copy.24
  130.1 31.0 %all_to_all.54 = f32[128,12,128]{2,1,0:T(8,128)S(1)} all-to-all(f32[128,12,128]{2,1,0:T(8,128)S(1)} %copy.24), channel_id=1, replica_groups=mesh['row'=4,'col'=8] {'col'}, dimensions={0} | all-to-all | bytes 1572864 | tf_op jit(solution)/shard_map/all_to_all | solution.py:12
  161.0 0.2 copy.25
  161.3 0.7 constant_dynamic-slice_fusion.1
  162.0 0.0 all-gather.6.cloned.1.call-update
  162.0 0.0 reduce-scatter.6.cloned.1.call-start
  162.0 23.3 %all-gather.6.cloned.1.call-done = f32[128,24,128]{2,0,1:T(8,128)} async-done(((f32[16,24,128]{2,0,1:T(8,128)}), f32[128,24,128]{2,0,1:T(8,128)}) %all-gather.6.cloned.1.call-update) | async-done | bytes 1572880 | tf_op jit(solution)/shard_map/all_gather | solution.py:14
  185.4 14.3 %fusion.9 = f32[128,12,128]{2,0,1:T(8,128)} fusion(f32[24,12,128,128]{3,2,1,0:T(8,128)} %param.4, f32[128,24,128]{2,0,1:T(8,128)} %all-gather.6.cloned.1.call-done), kind=kOutput, calls=%fused_computation.7 | convolution fusion | flops 7247757312 | bytes 21233664 | tf_op jit(solution)/shard_map/isl,stlj->itj/dot_general | solution.py:18
  199.6 0.0 reduce-scatter.6.cloned.1.call-update
  199.6 0.0 all-gather.8.cloned.1.call-start
  199.7 25.4 %reduce-scatter.6.cloned.1.call-done = f32[32,12,128]{2,0,1:T(8,128)} async-done(((f32[128,12,128]{2,0,1:T(8,128)}), f32[32,12,128]{2,0,1:T(8,128)}) %reduce-scatter.6.cloned.1.call-update) | async-done | bytes 196624 | tf_op jit(solution)/shard_map/reduce_scatter | solution.py:46
  225.1 1.2 multiply_multiply_fusion
  226.3 11.2 %all_gather.22 = f32[128,12,128]{2,0,1:T(8,128)S(1)} all-gather(f32[32,12,128]{2,0,1:T(8,128)S(1)} %get-tuple-element.7), channel_id=1, replica_groups=mesh['row'=4,'col'=8] {'row'}, dimensions={0}, use_global_device_ids=true | all-gather | bytes 983040 | tf_op jit(solution)/shard_map/all_gather | solution.py:44
  237.5 0.5 copy.27
  238.0 31.0 %all_to_all.55 = f32[128,12,128]{2,1,0:T(8,128)S(1)} all-to-all(f32[128,12,128]{2,1,0:T(8,128)S(1)} %copy.27), channel_id=1, replica_groups=mesh['row'=4,'col'=8] {'col'}, dimensions={0} | all-to-all | bytes 1572864 | tf_op jit(solution)/shard_map/all_to_all | solution.py:12
  268.9 0.2 copy.28
  269.2 0.7 constant_dynamic-slice_fusion
  269.9 0.0 all-gather.8.cloned.1.call-update
  269.9 0.2 reduce-scatter.8.cloned.1.call-start
  270.1 23.1 %all-gather.8.cloned.1.call-done = f32[128,24,128]{2,0,1:T(8,128)} async-done(((f32[16,24,128]{2,0,1:T(8,128)}), f32[128,24,128]{2,0,1:T(8,128)}) %all-gather.8.cloned.1.call-update) | async-done | bytes 1572880 | tf_op jit(solution)/shard_map/all_gather | solution.py:14
  293.3 14.3 %fusion.12 = f32[128,12,128]{2,0,1:T(8,128)} fusion(f32[24,12,128,128]{3,2,1,0:T(8,128)} %param.4, f32[128,24,128]{2,0,1:T(8,128)} %all-gather.8.cloned.1.call-done), kind=kOutput, calls=%fused_computation.8 | convolution fusion | flops 7247757312 | bytes 21233664 | tf_op jit(solution)/shard_map/isl,stlj->itj/dot_general | solution.py:18
  307.5 0.0 reduce-scatter.8.cloned.1.call-update
  307.6 25.4 %reduce-scatter.8.cloned.1.call-done = f32[32,12,128]{2,0,1:T(8,128)} async-done(((f32[128,12,128]{2,0,1:T(8,128)}), f32[32,12,128]{2,0,1:T(8,128)}) %reduce-scatter.8.cloned.1.call-update) | async-done | bytes 196624 | tf_op jit(solution)/shard_map/reduce_scatter | solution.py:46
  333.0 1.2 fusion.17
  334.2 0.9 pad_maximum_fusion
Async XLA Ops:
  6.5 110.6 %copy-start = (f32[128,128]{1,0:T(8,128)S(1)}, f32[128,128]{1,0:T(8,128)}, u32[]{:S(2)}) copy-start(f32[128,128]{1,0:T(8,128)} %param.5) | copy-start | bytes 196612
  21.6 31.4 %all-to-all-start = ((f32[128,12,128]{2,1,0:T(8,128)}), f32[128,12,128]{2,1,0:T(8,128)S(1)}, u32[]{:S(2)}, u32[]{:S(2)}) async-start(f32[128,12,128]{2,1,0:T(8,128)} %copy.21), calls=%async_computation | async-start | bytes 2097152 | tf_op jit(solution)/shard_map/all_to_all | solution.py:12
  26.5 50.9 %all-gather.4.cloned.1.call-start = ((), (), s32[]{:S(2)}) async-start(), calls=%async_computation.6 | async-start | bytes 1769472 | tf_op jit(solution)/shard_map/all_gather | solution.py:14
  54.1 63.1 %copy-start.1 = (f32[32,12,128]{2,0,1:T(8,128)S(1)}, f32[32,12,128]{2,0,1:T(8,128)}, u32[]{:S(2)}) copy-start(f32[32,12,128]{2,0,1:T(8,128)} %param.3) | copy-start | bytes 589828
  54.1 63.1 %reduce-scatter.4.cloned.1.call-start = ((), (), s32[]{:S(2)}) async-start(), calls=%async_computation.7 | async-start | bytes 983040 | tf_op jit(solution)/shard_map/reduce_scatter | solution.py:46
  91.7 93.6 %all-gather.6.cloned.1.call-start = ((), (), s32[]{:S(2)}) async-start(), calls=%async_computation.8 | async-start | bytes 1769472 | tf_op jit(solution)/shard_map/all_gather | solution.py:14
  162.0 63.1 %reduce-scatter.6.cloned.1.call-start = ((), (), s32[]{:S(2)}) async-start(), calls=%async_computation.9 | async-start | bytes 983040 | tf_op jit(solution)/shard_map/reduce_scatter | solution.py:46
  199.6 93.6 %all-gather.8.cloned.1.call-start = ((), (), s32[]{:S(2)}) async-start(), calls=%async_computation.10 | async-start | bytes 1769472 | tf_op jit(solution)/shard_map/all_gather | solution.py:14
  269.9 63.1 %reduce-scatter.8.cloned.1.call-start = ((), (), s32[]{:S(2)}) async-start(), calls=%async_computation.11 | async-start | bytes 983040 | tf_op jit(solution)/shard_map/reduce_scatter | solution.py:46
Sparse Core Ops, SparseCore 0:
  54.2 23.2 all-gather.3
  91.9 25.2 reduce-scatter.3
  162.1 23.2 all-gather.5
  199.8 25.2 reduce-scatter.5
  270.0 23.2 all-gather.7
  307.7 25.2 reduce-scatter.7
where the time goes:
time: 342 us
  waiting for transfers between devices  173 us (51%)
  blocking collectives  96.9 us (28%)
  matrix products  46.5 us (14%)
  between operations  13.5 us (4%)
  starting transfers between devices  5.3 us (2%)
  local copies, waits for them, and re-layouts  5.23 us (2%)
    reduce_scatter x3, waiting for transfers between devices, per_device(): lax.psum_scatter(contract(sigma_rows, history), 'row', scatter_dimension=...  76.2 us
    all_gather x3, waiting for transfers between devices, sigma_panel(): return lax.all_gather(needed, 'col', axis=0, tiled=True)  69.8 us
    all_to_all x2, blocking collectives, sigma_panel(): lax.all_to_all(sigma_all, 'col', split_axis=0, concat_axis=1, tiled=True)  61.9 us
    dot_general x3, matrix products, contract(): jnp.einsum('isl,stlj->itj', sigma_rows, history, precision=lax.Precision....  42.8 us
    all_gather x3, blocking collectives, per_device(): sigma_all = lax.all_gather(sigma_local, 'row', axis=0, tiled=True)  35 us
    all_to_all x1, waiting for transfers between devices, sigma_panel(): lax.all_to_all(sigma_all, 'col', split_axis=0, concat_axis=1, tiled=True)  26.5 us
  transfers between devices with their start and end apart: 7, of which 7 were waited for; matrix products, arithmetic and copies ran while one was open for 0% of the time, Pallas kernels for 0%

commit v1 on v0

--- a/solution.py
+++ b/solution.py
@@ -7,9 +7,16 @@
 time_step = 0.2
 
 
+def trade_parts(array, axis, split, join):
+    size = lax.axis_size(axis)
+    tiles = jnp.stack(jnp.split(array, size, axis=split), axis=0)
+    tiles = lax.all_to_all(tiles, axis, split_axis=0, concat_axis=0)
+    return jnp.concatenate(tiles, axis=join)
+
+
 def sigma_panel(sigma_all, tile_rows):
     row_start = lax.axis_index("row") * tile_rows
-    pieces = lax.all_to_all(sigma_all, "col", split_axis=0, concat_axis=1, tiled=True)
+    pieces = trade_parts(sigma_all, "col", 0, 1)
     needed = lax.dynamic_slice_in_dim(pieces, row_start, tile_rows, 1)
     return lax.all_gather(needed, "col", axis=0, tiled=True)
 

time: 342 us -> 328 us (0.959)
  blocking collectives: 96.9 us -> 85.7 us
  waiting for transfers between devices: 173 us -> 167 us
    all_to_all x2, blocking collectives: 61.9 us -> 50.7 us  [trade_parts(): tiles = lax.all_to_all(tiles, axis, split_axis=0, concat_axis=0)]
    all_to_all x1, waiting for transfers between devices: 26.5 us -> 20.9 us  [trade_parts(): tiles = lax.all_to_all(tiles, axis, split_axis=0, concat_axis=0)]
    unnamed x4 -> x25, local copies, waits for them, and re-layouts: 0.01 us -> 4.62 us
where the time goes in v1:
time: 328 us; the launch traced here: 327 us
  waiting for transfers between devices  167 us (51%)
  blocking collectives  85.7 us (26%)
  matrix products  46.5 us (14%)
  between operations  13.7 us (4%)
  local copies, waits for them, and re-layouts  7.37 us (2%)
  starting transfers between devices  5.3 us (2%)
    reduce_scatter x3, waiting for transfers between devices, per_device(): lax.psum_scatter(contract(sigma_rows, history), 'row', scatter_dimension=...  76.2 us
    all_gather x3, waiting for transfers between devices, sigma_panel(): return lax.all_gather(needed, 'col', axis=0, tiled=True)  69.8 us
    all_to_all x2, blocking collectives, trade_parts(): tiles = lax.all_to_all(tiles, axis, split_axis=0, concat_axis=0)  50.7 us
    dot_general x3, matrix products, contract(): jnp.einsum('isl,stlj->itj', sigma_rows, history, precision=lax.Precision....  42.8 us
    all_gather x3, blocking collectives, per_device(): sigma_all = lax.all_gather(sigma_local, 'row', axis=0, tiled=True)  35 us
    all_to_all x1, waiting for transfers between devices, trade_parts(): tiles = lax.all_to_all(tiles, axis, split_axis=0, concat_axis=0)  20.9 us
  transfers between devices with their start and end apart: 7, of which 7 were waited for; matrix products, arithmetic and copies ran while one was open for 0% of the time, Pallas kernels for 0%

profile of v1, /device:TPU:0, one launch (start us, length us, event | category | flops | bytes accessed | tf_op | source)
XLA Modules:
  0.0 327.3 jit_solution(3410378541279731374)
XLA Ops:
  6.5 0.0 copy-start
  6.5 1.0 multiply_multiply_fusion.2
  7.5 12.7 %all_gather.18 = f32[128,12,128]{2,0,1:T(8,128)S(1)} all-gather(f32[32,12,128]{2,0,1:T(8,128)S(1)} %multiply_multiply_fusion.2), channel_id=1, replica_groups=mesh['row'=4,'col'=8] {'row'}, dimensions={0}, use_global_device_ids=true | all-gather | bytes 983040 | tf_op jit(solution)/shard_map/all_gather | solution.py:51
  20.2 0.6 fusion.45
  20.8 0.6 fusion.44
  21.5 0.6 fusion.43
  22.1 0.6 fusion.42
  22.8 0.6 fusion.41
  23.4 0.6 fusion.40
  24.0 0.6 fusion.39
  24.7 0.7 fusion.38
  25.3 4.9 %all-to-all-start = ((f32[8,16,12,128]{3,1,2,0:T(8,128)}), f32[8,16,12,128]{3,1,2,0:T(8,128)S(1)}, u32[]{:S(2)}, u32[]{:S(2)}) async-start(f32[8,16,12,128]{3,1,2,0:T(8,128)} %fusion.38), calls=%async_computation | async-start | bytes 1572864 | tf_op jit(solution)/shard_map/all_to_all | solution.py:13
  30.2 0.0 all-gather.4.cloned.1.call-start
  30.3 20.9 %all-to-all-done = f32[8,16,12,128]{3,1,2,0:T(8,128)S(1)} async-done(((f32[8,16,12,128]{3,1,2,0:T(8,128)}), f32[8,16,12,128]{3,1,2,0:T(8,128)S(1)}, u32[]{:S(2)}, u32[]{:S(2)}) %all-to-all-start) | async-done | bytes 786464 | tf_op jit(solution)/shard_map/all_to_all | solution.py:13
  51.2 0.7 constant_dynamic-slice_fusion.2
  51.9 0.0 all-gather.4.cloned.1.call-update
  51.9 0.0 copy-start.1
  51.9 0.0 reduce-scatter.4.cloned.1.call-start
  51.9 23.3 %all-gather.4.cloned.1.call-done = f32[128,24,128]{2,0,1:T(8,128)} async-done(((f32[16,24,128]{2,0,1:T(8,128)}), f32[128,24,128]{2,0,1:T(8,128)}) %all-gather.4.cloned.1.call-update) | async-done | bytes 1572880 | tf_op jit(solution)/shard_map/all_gather | solution.py:21
  75.3 14.3 %fusion.6 = f32[128,12,128]{2,0,1:T(8,128)} fusion(f32[24,12,128,128]{3,2,1,0:T(8,128)} %param.4, f32[128,24,128]{2,0,1:T(8,128)} %all-gather.4.cloned.1.call-done), kind=kOutput, calls=%fused_computation.6 | convolution fusion | flops 7247757312 | bytes 21233664 | tf_op jit(solution)/shard_map/isl,stlj->itj/dot_general | solution.py:25
  89.5 0.0 reduce-scatter.4.cloned.1.call-update
  89.6 0.0 all-gather.6.cloned.1.call-start
  89.6 25.4 %reduce-scatter.4.cloned.1.call-done = f32[32,12,128]{2,0,1:T(8,128)} async-done(((f32[128,12,128]{2,0,1:T(8,128)}), f32[32,12,128]{2,0,1:T(8,128)}) %reduce-scatter.4.cloned.1.call-update) | async-done | bytes 196624 | tf_op jit(solution)/shard_map/reduce_scatter | solution.py:53
  115.0 0.0 copy-done
  115.0 0.0 copy-done.1
  115.0 1.2 multiply_multiply_fusion.1
  116.3 11.2 %all_gather.20 = f32[128,12,128]{2,0,1:T(8,128)S(1)} all-gather(f32[32,12,128]{2,0,1:T(8,128)S(1)} %get-tuple-element.5), channel_id=1, replica_groups=mesh['row'=4,'col'=8] {'row'}, dimensions={0}, use_global_device_ids=true | all-gather | bytes 983040 | tf_op jit(solution)/shard_map/all_gather | solution.py:51
  127.6 25.3 %all_to_all.15 = f32[8,16,12,128]{3,1,2,0:T(8,128)S(1)} all-to-all(f32[8,16,12,128]{3,1,2,0:T(8,128)S(1)} %fusion.30), channel_id=1, replica_groups=mesh['row'=4,'col'=8] {'col'}, dimensions={0} | all-to-all | bytes 1572864 | tf_op jit(solution)/shard_map/all_to_all | solution.py:13
  152.9 0.7 constant_dynamic-slice_fusion.1
  153.6 0.0 all-gather.6.cloned.1.call-update
  153.6 0.0 reduce-scatter.6.cloned.1.call-start
  153.7 23.3 %all-gather.6.cloned.1.call-done = f32[128,24,128]{2,0,1:T(8,128)} async-done(((f32[16,24,128]{2,0,1:T(8,128)}), f32[128,24,128]{2,0,1:T(8,128)}) %all-gather.6.cloned.1.call-update) | async-done | bytes 1572880 | tf_op jit(solution)/shard_map/all_gather | solution.py:21
  177.0 14.2 %fusion.9 = f32[128,12,128]{2,0,1:T(8,128)} fusion(f32[24,12,128,128]{3,2,1,0:T(8,128)} %param.4, f32[128,24,128]{2,0,1:T(8,128)} %all-gather.6.cloned.1.call-done), kind=kOutput, calls=%fused_computation.7 | convolution fusion | flops 7247757312 | bytes 21233664 | tf_op jit(solution)/shard_map/isl,stlj->itj/dot_general | solution.py:25
  191.2 0.0 reduce-scatter.6.cloned.1.call-update
  191.3 0.0 all-gather.8.cloned.1.call-start
  191.3 25.4 %reduce-scatter.6.cloned.1.call-done = f32[32,12,128]{2,0,1:T(8,128)} async-done(((f32[128,12,128]{2,0,1:T(8,128)}), f32[32,12,128]{2,0,1:T(8,128)}) %reduce-scatter.6.cloned.1.call-update) | async-done | bytes 196624 | tf_op jit(solution)/shard_map/reduce_scatter | solution.py:53
  216.7 1.2 multiply_multiply_fusion
  218.0 11.2 %all_gather.22 = f32[128,12,128]{2,0,1:T(8,128)S(1)} all-gather(f32[32,12,128]{2,0,1:T(8,128)S(1)} %get-tuple-element.7), channel_id=1, replica_groups=mesh['row'=4,'col'=8] {'row'}, dimensions={0}, use_global_device_ids=true | all-gather | bytes 983040 | tf_op jit(solution)/shard_map/all_gather | solution.py:51
  229.3 25.3 %all_to_all.16 = f32[8,16,12,128]{3,1,2,0:T(8,128)S(1)} all-to-all(f32[8,16,12,128]{3,1,2,0:T(8,128)S(1)} %fusion.22), channel_id=1, replica_groups=mesh['row'=4,'col'=8] {'col'}, dimensions={0} | all-to-all | bytes 1572864 | tf_op jit(solution)/shard_map/all_to_all | solution.py:13
  254.6 0.7 constant_dynamic-slice_fusion
  255.3 0.0 all-gather.8.cloned.1.call-update
  255.3 0.2 reduce-scatter.8.cloned.1.call-start
  255.5 23.1 %all-gather.8.cloned.1.call-done = f32[128,24,128]{2,0,1:T(8,128)} async-done(((f32[16,24,128]{2,0,1:T(8,128)}), f32[128,24,128]{2,0,1:T(8,128)}) %all-gather.8.cloned.1.call-update) | async-done | bytes 1572880 | tf_op jit(solution)/shard_map/all_gather | solution.py:21
  278.7 14.2 %fusion.12 = f32[128,12,128]{2,0,1:T(8,128)} fusion(f32[24,12,128,128]{3,2,1,0:T(8,128)} %param.4, f32[128,24,128]{2,0,1:T(8,128)} %all-gather.8.cloned.1.call-done), kind=kOutput, calls=%fused_computation.8 | convolution fusion | flops 7247757312 | bytes 21233664 | tf_op jit(solution)/shard_map/isl,stlj->itj/dot_general | solution.py:25
  292.9 0.0 reduce-scatter.8.cloned.1.call-update
  293.0 25.4 %reduce-scatter.8.cloned.1.call-done = f32[32,12,128]{2,0,1:T(8,128)} async-done(((f32[128,12,128]{2,0,1:T(8,128)}), f32[32,12,128]{2,0,1:T(8,128)}) %reduce-scatter.8.cloned.1.call-update) | async-done | bytes 196624 | tf_op jit(solution)/shard_map/reduce_scatter | solution.py:53
  318.4 1.2 fusion.17
  319.6 0.9 pad_maximum_fusion
  (16 shorter events, 0.1 us)
Async XLA Ops:
  6.5 108.5 %copy-start = (f32[128,128]{1,0:T(8,128)S(1)}, f32[128,128]{1,0:T(8,128)}, u32[]{:S(2)}) copy-start(f32[128,128]{1,0:T(8,128)} %param.5) | copy-start | bytes 196612
  25.3 25.8 %all-to-all-start = ((f32[8,16,12,128]{3,1,2,0:T(8,128)}), f32[8,16,12,128]{3,1,2,0:T(8,128)S(1)}, u32[]{:S(2)}, u32[]{:S(2)}) async-start(f32[8,16,12,128]{3,1,2,0:T(8,128)} %fusion.38), calls=%async_computation | async-start | bytes 1572864 | tf_op jit(solution)/shard_map/all_to_all | solution.py:13
  30.2 45.1 %all-gather.4.cloned.1.call-start = ((), (), s32[]{:S(2)}) async-start(), calls=%async_computation.6 | async-start | bytes 1769472 | tf_op jit(solution)/shard_map/all_gather | solution.py:21
  51.9 63.1 %copy-start.1 = (f32[32,12,128]{2,0,1:T(8,128)S(1)}, f32[32,12,128]{2,0,1:T(8,128)}, u32[]{:S(2)}) copy-start(f32[32,12,128]{2,0,1:T(8,128)} %param.3) | copy-start | bytes 589828
  51.9 63.1 %reduce-scatter.4.cloned.1.call-start = ((), (), s32[]{:S(2)}) async-start(), calls=%async_computation.7 | async-start | bytes 983040 | tf_op jit(solution)/shard_map/reduce_scatter | solution.py:53
  89.6 87.4 %all-gather.6.cloned.1.call-start = ((), (), s32[]{:S(2)}) async-start(), calls=%async_computation.8 | async-start | bytes 1769472 | tf_op jit(solution)/shard_map/all_gather | solution.py:21
  153.6 63.1 %reduce-scatter.6.cloned.1.call-start = ((), (), s32[]{:S(2)}) async-start(), calls=%async_computation.9 | async-start | bytes 983040 | tf_op jit(solution)/shard_map/reduce_scatter | solution.py:53
  191.3 87.4 %all-gather.8.cloned.1.call-start = ((), (), s32[]{:S(2)}) async-start(), calls=%async_computation.10 | async-start | bytes 1769472 | tf_op jit(solution)/shard_map/all_gather | solution.py:21
  255.3 63.1 %reduce-scatter.8.cloned.1.call-start = ((), (), s32[]{:S(2)}) async-start(), calls=%async_computation.11 | async-start | bytes 983040 | tf_op jit(solution)/shard_map/reduce_scatter | solution.py:53
Sparse Core Ops, SparseCore 0:
  52.0 23.2 all-gather.3
  89.7 25.2 reduce-scatter.3
  153.7 23.2 all-gather.5
  191.4 25.2 reduce-scatter.5
  255.4 23.2 all-gather.7
  293.1 25.2 reduce-scatter.7
